TPU v7x, 128 devices: a whole 4x4x4 slice. The times are simulated.
128 devices in a mesh: kv: 32 (over y, z, x_hi), pb: 4 (over x_lo, core).
Axes of the slice: x: 4 (x_hi: 2, x_lo: 2; x = x_hi * 2 + x_lo), y: 4, z: 4, core: 2. Of those that a mesh axis runs over, the one named last changes fastest.
Arguments:
- queries: bfloat16 [49152, 4096], P('kv', 'pb'), may hold values from -12 to 12
- cached_keys: bfloat16 [32, 256, 4096], P('kv', None, 'pb'), may hold values from -6 to 6
- cached_values: bfloat16 [32, 256, 4096], P('kv', None, 'pb'), may hold values from -6 to 6
- block_map: int32 [768, 1], P('kv'), may hold values from 0 to 31; in each aligned block of 24 rows (0 to 23, 24 to 47, ...) at most 2 rows name the same one
- out_weight: bfloat16 [4096, 4096], P('pb'), may hold values from -0.09375 to 0.09375
- hidden: bfloat16 [49152, 4096], P('kv', 'pb'), may hold values from -6 to 6
Outputs:
- mixed: bfloat16 [49152, 4096], P('kv', 'pb')
Inputs may be any that keep to these rules, and one draw needn't show every extreme that they name: `block_map`: at most 2 of the 24 spans of one index of kv name the same block, and some index has a block named by exactly 2 of its spans; every block is named by some span.
All inputs are finite; a program needn't handle non-finite values.
Results may differ from a plain program's by a relative error of at most 0.0085.
Values may be sent and summed in bfloat16 or wider, within the bound.
No kernel may reach another device: no remote copies, remote signals or barrier semaphores. Data moves between devices by JAX's collectives and lax.ppermute only.
A program may use at most 192 MiB of HBM per device.

v0:
```python
import jax
import jax.numpy as jnp
from jax import lax
from jax.sharding import PartitionSpec as P

HEAD = 128
SPAN = 64


def attend(span_queries, keys_now, values_now):
    item_count, row_count, feat_width = span_queries.shape
    key_count = keys_now.shape[0]
    head_count = feat_width // HEAD
    query_heads = span_queries.reshape(item_count, row_count, head_count, HEAD)
    key_heads = keys_now.reshape(key_count, head_count, HEAD)
    value_heads = values_now.reshape(key_count, head_count, HEAD)
    scores = jnp.einsum(
        "nrhd,khd->nhrk", query_heads, key_heads, preferred_element_type=jnp.float32
    ) * HEAD ** (-0.5)
    row_top = jnp.max(scores, axis=-1, keepdims=True)
    exponent = jnp.exp(scores - row_top)
    weights = (exponent / jnp.sum(exponent, axis=-1, keepdims=True)).astype(jnp.bfloat16)
    result = jnp.einsum("nhrk,khd->nrhd", weights, value_heads, preferred_element_type=jnp.float32)
    return result.reshape(item_count, row_count, feat_width).astype(jnp.bfloat16)


def on_device(queries, cached_keys, cached_values, block_map, out_weight, hidden):
    tok_rows, feat_width = queries.shape
    span_count = tok_rows // SPAN
    q_spans = queries.reshape(span_count, SPAN, feat_width)
    block_count = lax.axis_size("kv")
    cap_slots = max(2, span_count // block_count)
    targets = block_map[:, 0]
    onehot = (targets[:, None] == jnp.arange(block_count, dtype=jnp.int32)[None, :]).astype(
        jnp.int32
    )
    earlier = jnp.cumsum(onehot, axis=0) - onehot
    position_in = jnp.sum(earlier * onehot, axis=1)
    slot_index = targets * cap_slots + position_in
    start_sum = jnp.zeros((span_count, SPAN, feat_width), jnp.float32)
    key_piece = lax.all_gather(cached_keys, "kv", axis=0, tiled=True)
    value_piece = lax.all_gather(cached_values, "kv", axis=0, tiled=True)

    def one_block(block_step, so_far):
        keys_now = lax.dynamic_index_in_dim(key_piece, block_step, 0, keepdims=False)
        values_now = lax.dynamic_index_in_dim(value_piece, block_step, 0, keepdims=False)
        wanted = block_step * cap_slots + jnp.arange(cap_slots, dtype=jnp.int32)
        picks = (slot_index[None, :] == wanted[:, None]).astype(jnp.bfloat16)
        chosen = jnp.einsum(
            "sc,crd->srd", picks, q_spans, preferred_element_type=jnp.float32
        ).astype(jnp.bfloat16)
        answer = attend(chosen, keys_now, values_now)
        return so_far + jnp.einsum("sc,srd->crd", picks, answer, preferred_element_type=jnp.float32)

    gathered_sum = lax.fori_loop(0, key_piece.shape[0], one_block, start_sum)
    attended = gathered_sum.astype(jnp.bfloat16)
    flat_rows = attended.reshape(tok_rows, feat_width)
    partial_value = jnp.dot(flat_rows, out_weight, preferred_element_type=jnp.float32)
    summed = lax.psum_scatter(
        partial_value.astype(jnp.bfloat16), "pb", scatter_dimension=1, tiled=True
    ).astype(jnp.float32)
    return (hidden.astype(jnp.float32) + summed).astype(jnp.bfloat16)


def solution(mesh):
    placed = (
        P("kv", "pb"),
        P("kv", None, "pb"),
        P("kv", None, "pb"),
        P("kv", None),
        P("pb", None),
        P("kv", "pb"),
    )
    return jax.shard_map(
        on_device, mesh=mesh, in_specs=placed, out_specs=P("kv", "pb"), check_vma=False
    )
```

profile of v0, /device:TPU:1, one launch (start us, length us, event | category | flops | bytes accessed | tf_op | source)
XLA Modules:
  0.0 1246.2 jit_solution(3254958065707537142)
XLA Ops:
  12.7 156.4 %all-gather.5.cloned.1.call-done = bf16[32,256,1024]{2,1,0:T(8,128)(2,1)} async-done(((bf16[1,256,1024]{2,1,0:T(8,128)(2,1)}), bf16[32,256,1024]{2,1,0:T(8,128)(2,1)}) %all-gather.5.cloned.1.call-update) | async-done | bytes 16777232 | tf_op jit(solution)/shard_map/all_gather | solution.py:41
  169.1 157.2 %all-gather.3.cloned.1.call-done = bf16[32,256,1024]{2,1,0:T(8,128)(2,1)} async-done(((bf16[1,256,1024]{2,1,0:T(8,128)(2,1)}), bf16[32,256,1024]{2,1,0:T(8,128)(2,1)}) %all-gather.3.cloned.1.call-update) | async-done | bytes 16777232 | tf_op jit(solution)/shard_map/all_gather | solution.py:42
  326.2 774.2 %while.14 = (s32[]{:T(128)}, f32[24,64,1024]{2,0,1:T(8,128)}, s32[24]{0:T(128)S(1)}, bf16[32,256,1024]{2,1,0:T(8,128)(2,1)}, bf16[32,256,1024]{2,1,0:T(8,128)(2,...) while((s32[]{:T(128)}, f32[24,64,1024]{2,0,1:T(8,128)}, ...), condition=%wide.region_5.6_spmd.clone, body=%wide.region_2.5_spmd.clone.sunk | while | flops 152045168 | bytes 31465844 | solution.py:55
  338.0 4.0 fusion.55
  343.9 4.7 select_add_fusion.2
  360.3 4.0 fusion.55
  366.2 6.6 select_add_fusion.2
  384.6 4.0 fusion.55
  390.5 6.6 select_add_fusion.2
  408.8 4.0 fusion.55
  414.7 6.6 select_add_fusion.2
  433.1 4.0 fusion.55
  439.0 6.6 select_add_fusion.2
  457.3 4.0 fusion.55
  463.2 6.6 select_add_fusion.2
  481.6 4.0 fusion.55
  487.5 6.6 select_add_fusion.2
  505.8 4.0 fusion.55
  511.7 6.6 select_add_fusion.2
  530.1 4.0 fusion.55
  536.0 6.6 select_add_fusion.2
  554.4 4.0 fusion.55
  560.2 6.6 select_add_fusion.2
  578.6 4.0 fusion.55
  584.5 6.6 select_add_fusion.2
  602.9 4.0 fusion.55
  608.8 6.6 select_add_fusion.2
  627.1 4.0 fusion.55
  633.0 6.6 select_add_fusion.2
  651.4 4.0 fusion.55
  657.3 6.6 select_add_fusion.2
  675.6 4.0 fusion.55
  681.5 6.6 select_add_fusion.2
  699.9 4.0 fusion.55
  705.8 6.6 select_add_fusion.2
  724.1 4.0 fusion.55
  730.0 6.6 select_add_fusion.2
  748.4 4.0 fusion.55
  754.3 6.6 select_add_fusion.2
  772.7 4.0 fusion.55
  778.6 6.6 select_add_fusion.2
  796.9 4.0 fusion.55
  802.8 6.6 select_add_fusion.2
  821.2 4.0 fusion.55
  827.1 6.6 select_add_fusion.2
  845.4 4.0 fusion.55
  851.3 6.6 select_add_fusion.2
  869.7 4.0 fusion.55
  875.6 6.6 select_add_fusion.2
  893.9 4.0 fusion.55
  899.8 6.6 select_add_fusion.2
  918.2 4.0 fusion.55
  924.1 6.6 select_add_fusion.2
  948.3 6.6 select_add_fusion.2
  972.6 6.6 select_add_fusion.2
  996.9 6.6 select_add_fusion.2
  1021.1 6.6 select_add_fusion.2
  1045.4 6.6 select_add_fusion.2
  1069.6 6.6 select_add_fusion.2
  1093.9 6.6 select_add_fusion.2
  1100.5 6.3 copy.35
  1106.8 15.7 %convolution_convert_fusion.2 = bf16[1536,4096]{1,0:T(8,128)(2,1)} fusion(bf16[1536,1024]{1,0:T(8,128)(2,1)S(1)} %bitcast.78, bf16[1024,4096]{1,0:T(8,128)(2,1)S(1)} %copy-done.3), kind=kOutput, calls=%fused_computation.27 | convolution fusion | flops 12891193344 | bytes 24117248 | tf_op jit(solution)/shard_map/dot_general | solution.py:58
  1122.5 112.0 %reduce-scatter.2.cloned.1.call-done = bf16[1536,1024]{1,0:T(8,128)(2,1)} async-done(((bf16[1536,4096]{1,0:T(8,128)(2,1)}), bf16[1536,1024]{1,0:T(8,128)(2,1)}) %reduce-scatter.2.cloned.1.call-update) | async-done | bytes 3145744 | tf_op jit(solution)/shard_map/reduce_scatter | solution.py:59
  1234.6 5.1 add_convert_fusion
  (441 shorter events, 470.4 us)
Async XLA Ops:
  6.5 5.9 copy-start.2
  6.5 162.5 %all-gather.5.cloned.1.call-start = ((), (), s32[]{:S(2)}) async-start(), calls=%async_computation.2 | async-start | bytes 17301504 | tf_op jit(solution)/shard_map/all_gather | solution.py:41
  7.3 319.0 %all-gather.3.cloned.1.call-start = ((), (), s32[]{:S(2)}) async-start(), calls=%async_computation.1 | async-start | bytes 17301504 | tf_op jit(solution)/shard_map/all_gather | solution.py:42
  8.0 1226.5 %reduce-scatter.2.cloned.1.call-start = ((), (), s32[]{:S(2)}) async-start(), calls=%async_computation.3 | async-start | bytes 15728640 | tf_op jit(solution)/shard_map/reduce_scatter | solution.py:59
  336.6 1.0 copy-start
  359.0 1.0 copy-start
  383.2 1.0 copy-start
  407.5 1.0 copy-start
  431.7 1.0 copy-start
  456.0 1.0 copy-start
  480.2 1.0 copy-start
  504.5 1.0 copy-start
  528.7 1.0 copy-start
  553.0 1.0 copy-start
  577.3 1.0 copy-start
  601.5 1.0 copy-start
  625.8 1.0 copy-start
  650.0 1.0 copy-start
  674.3 1.0 copy-start
  698.5 1.0 copy-start
  722.8 1.0 copy-start
  747.1 1.0 copy-start
  771.3 1.0 copy-start
  795.6 1.0 copy-start
  819.8 1.0 copy-start
  844.1 1.0 copy-start
  868.3 1.0 copy-start
  892.6 1.0 copy-start
  916.8 1.0 copy-start
  941.1 1.0 copy-start
  965.3 1.0 copy-start
  989.6 1.0 copy-start
  1013.9 1.0 copy-start
  1038.1 1.0 copy-start
  1062.4 1.0 copy-start
  1086.6 1.0 copy-start
  1100.5 6.3 copy-start.3
  1122.5 112.1 %copy-start.1 = (bf16[1536,1024]{1,0:T(8,128)(2,1)S(1)}, bf16[1536,1024]{1,0:T(8,128)(2,1)}, u32[]{:S(2)}) copy-start(bf16[1536,1024]{1,0:T(8,128)(2,1)} %param.13) | copy-start | bytes 9437188
Sparse Core Ops, SparseCore 0:
  10.4 158.6 all-gather.4
  172.1 154.0 all-gather.2
  1122.6 111.8 reduce-scatter.1
where the time goes:
time: 1260 us; the launch traced here: 1250 us
  waiting for transfers between devices  427 us (34%)
  matrix products  420 us (33%)
  local copies, waits for them, and re-layouts  366 us (29%)
  other arithmetic  18.7 us (1%)
  between operations  13.1 us (1%)
    dot_general x32, matrix products, one_block(): jnp.einsum('sc,srd->crd', picks, answer, preferred_element_type=jnp.float32)  209 us
    all_gather x1, waiting for transfers between devices, on_device(): value_piece = lax.all_gather(cached_values, 'kv', axis=0, tiled=True)  157 us
    all_gather x1, waiting for transfers between devices, on_device(): key_piece = lax.all_gather(cached_keys, 'kv', axis=0, tiled=True)  156 us
    dynamic_slice x64, local copies, waits for them, and re-layouts, one_block(): lax.dynamic_index_in_dim(key_piece, block_step, 0, keepdims=False)  139 us
    dot_general x32, matrix products, attend(): jnp.einsum('nhrk,khd->nrhd', weights, value_heads, preferred_element_type...  128 us
    reduce_scatter x1, waiting for transfers between devices, on_device(): lax.psum_scatter(partial_value.astype(jnp.bfloat16), 'pb', scatter_dimens...  112 us
    dynamic_slice x32, local copies, waits for them, and re-layouts, one_block(): lax.dynamic_index_in_dim(value_piece, block_step, 0, keepdims=False)  66.1 us
    reshape x64, local copies, waits for them, and re-layouts, attend(): query_heads = span_queries.reshape(item_count, row_count, head_count, HEAD)  60.5 us
  transfers between devices with their start and end apart: 3, of which 3 were waited for; matrix products, arithmetic and copies ran while one was open for 0% of the time, Pallas kernels for 0%

commit v1 on v0

--- a/solution.py
+++ b/solution.py
@@ -39,7 +39,10 @@
     slot_index = targets * cap_slots + position_in
     start_sum = jnp.zeros((span_count, SPAN, feat_width), jnp.float32)
     key_piece = lax.all_gather(cached_keys, "kv", axis=0, tiled=True)
-    value_piece = lax.all_gather(cached_values, "kv", axis=0, tiled=True)
+    devices = lax.axis_size("kv")
+    parts = jnp.stack([cached_values for _ in range(devices)])
+    parts = lax.all_to_all(parts, "kv", split_axis=0, concat_axis=0)
+    value_piece = jnp.concatenate(parts, axis=0)
 
     def one_block(block_step, so_far):
         keys_now = lax.dynamic_index_in_dim(key_piece, block_step, 0, keepdims=False)

time: 1260 us -> 1330 us (1.056)
  waiting for transfers between devices: 427 us -> 498 us
    all_to_all x0 -> x1, waiting for transfers between devices: none -> 261 us  [on_device(): parts = lax.all_to_all(parts, 'kv', split_axis=0, concat_axis=0)]
    all_gather x1 -> x0, waiting for transfers between devices: 157 us -> none  [on_device(): value_piece = lax.all_gather(cached_values, 'kv', axis=0, tiled=True)]
    all_gather x1, waiting for transfers between devices: 156 us -> 109 us  [on_device(): key_piece = lax.all_gather(cached_keys, 'kv', axis=0, tiled=True)]
    reduce_scatter x1, waiting for transfers between devices: 112 us -> 127 us  [on_device(): lax.psum_scatter(partial_value.astype(jnp.bfloat16), 'pb', scatter_dimens...]
  transfers between devices with their start and end apart: 3 -> 3, of which waited for: 3 -> 3; matrix products, arithmetic and copies ran while one was open for 0% -> 1% of each run, Pallas kernels for 0% -> 0%
where the time goes in v1:
time: 1330 us; the launch traced here: 1320 us
  waiting for transfers between devices  498 us (37%)
  matrix products  423 us (32%)
  local copies, waits for them, and re-layouts  354 us (27%)
  other arithmetic  18 us (1%)
  between operations  13.4 us (1%)
    all_to_all x1, waiting for transfers between devices, on_device(): parts = lax.all_to_all(parts, 'kv', split_axis=0, concat_axis=0)  261 us
    dot_general x32, matrix products, one_block(): jnp.einsum('sc,srd->crd', picks, answer, preferred_element_type=jnp.float32)  209 us
    dot_general x32, matrix products, attend(): jnp.einsum('nhrk,khd->nrhd', weights, value_heads, preferred_element_type...  128 us
    reduce_scatter x1, waiting for transfers between devices, on_device(): lax.psum_scatter(partial_value.astype(jnp.bfloat16), 'pb', scatter_dimens...  127 us
    dynamic_slice x64, local copies, waits for them, and re-layouts, one_block(): lax.dynamic_index_in_dim(key_piece, block_step, 0, keepdims=False)  125 us
    all_gather x1, waiting for transfers between devices, on_device(): key_piece = lax.all_gather(cached_keys, 'kv', axis=0, tiled=True)  109 us
    convert_element_type x64, local copies, waits for them, and re-layouts, attend(): result.reshape(item_count, row_count, feat_width).astype(jnp.bfloat16)  60.5 us
    reshape x64, local copies, waits for them, and re-layouts, attend(): query_heads = span_queries.reshape(item_count, row_count, head_count, HEAD)  60.5 us
  transfers between devices with their start and end apart: 3, of which 3 were waited for; matrix products, arithmetic and copies ran while one was open for 1% of the time, Pallas kernels for 0%

profile of v1, /device:TPU:1, one launch (start us, length us, event | category | flops | bytes accessed | tf_op | source)
XLA Modules:
  0.0 1318.9 jit_solution(1254690653540541889)
XLA Ops:
  8.5 5.9 stack.2
  14.4 11.6 all-to-all-start
  30.0 261.2 %all-to-all-done = bf16[32,1,256,1024]{2,3,1,0:T(8,128)(2,1)} async-done(((bf16[32,1,256,1024]{2,3,1,0:T(8,128)(2,1)}), bf16[32,1,256,1024]{2,3,1,0:T(8,128)(2,1)}, u32[]{:S(2)}, u32[]{:S(2)}) %all-to-all-start) | async-done | bytes 16777248 | tf_op jit(solution)/shard_map/all_to_all | solution.py:44
  291.3 108.9 %all-gather.2.cloned.1.call-done = bf16[32,256,1024]{2,1,0:T(8,128)(2,1)} async-done(((bf16[1,256,1024]{2,1,0:T(8,128)(2,1)}), bf16[32,256,1024]{2,1,0:T(8,128)(2,1)}) %all-gather.2.cloned.1.call-update) | async-done | bytes 16777232 | tf_op jit(solution)/shard_map/all_gather | solution.py:41
  400.1 754.6 %while.14 = (s32[]{:T(128)}, f32[24,64,1024]{2,0,1:T(8,128)}, s32[24]{0:T(128)S(1)}, bf16[32,256,1024]{1,2,0:T(8,128)(2,1)}, bf16[32,256,1024]{2,1,0:T(8,128)(2,...) while((s32[]{:T(128)}, f32[24,64,1024]{2,0,1:T(8,128)}, ...), condition=%wide.region_5.6_spmd.clone, body=%wide.region_2.5_spmd.clone.sunk | while | flops 152045168 | bytes 30417264 | solution.py:58
  411.3 4.0 fusion.55
  417.2 4.7 select_add_fusion.2
  433.0 4.0 fusion.55
  438.9 6.6 select_add_fusion.2
  456.6 4.0 fusion.55
  462.5 6.6 select_add_fusion.2
  480.3 4.0 fusion.55
  486.2 6.6 select_add_fusion.2
  503.9 4.0 fusion.55
  509.8 6.6 select_add_fusion.2
  527.6 4.0 fusion.55
  533.5 6.6 select_add_fusion.2
  551.2 4.0 fusion.55
  557.1 6.6 select_add_fusion.2
  574.8 4.0 fusion.55
  580.7 6.6 select_add_fusion.2
  598.5 4.0 fusion.55
  604.4 6.6 select_add_fusion.2
  622.1 4.0 fusion.55
  628.0 6.6 select_add_fusion.2
  645.8 4.0 fusion.55
  651.7 6.6 select_add_fusion.2
  669.4 4.0 fusion.55
  675.3 6.6 select_add_fusion.2
  693.1 4.0 fusion.55
  698.9 6.6 select_add_fusion.2
  716.7 4.0 fusion.55
  722.6 6.6 select_add_fusion.2
  740.3 4.0 fusion.55
  746.2 6.6 select_add_fusion.2
  764.0 4.0 fusion.55
  769.9 6.6 select_add_fusion.2
  787.6 4.0 fusion.55
  793.5 6.6 select_add_fusion.2
  811.3 4.0 fusion.55
  817.1 6.6 select_add_fusion.2
  834.9 4.0 fusion.55
  840.8 6.6 select_add_fusion.2
  858.5 4.0 fusion.55
  864.4 6.6 select_add_fusion.2
  882.2 4.0 fusion.55
  888.1 6.6 select_add_fusion.2
  905.8 4.0 fusion.55
  911.7 6.6 select_add_fusion.2
  929.5 4.0 fusion.55
  935.3 6.6 select_add_fusion.2
  959.0 6.6 select_add_fusion.2
  982.6 6.6 select_add_fusion.2
  1006.3 6.6 select_add_fusion.2
  1029.9 6.6 select_add_fusion.2
  1053.5 6.6 select_add_fusion.2
  1077.2 6.6 select_add_fusion.2
  1100.8 6.6 select_add_fusion.2
  1124.5 6.6 select_add_fusion.2
  1148.1 6.6 select_add_fusion.2
  1154.7 6.1 copy.34
  1160.8 18.8 %convolution_convert_fusion.2 = bf16[1536,4096]{1,0:T(8,128)(2,1)} fusion(bf16[1536,1024]{1,0:T(8,128)(2,1)S(1)} %bitcast.80, bf16[1024,4096]{1,0:T(8,128)(2,1)} %param.12), kind=kOutput, calls=%fused_computation.27 | convolution fusion | flops 12891193344 | bytes 24117248 | tf_op jit(solution)/shard_map/dot_general | solution.py:61
  1179.6 127.3 %reduce-scatter.2.cloned.1.call-done = bf16[1536,1024]{1,0:T(8,128)(2,1)} async-done(((bf16[1536,4096]{1,0:T(8,128)(2,1)}), bf16[1536,1024]{1,0:T(8,128)(2,1)}) %reduce-scatter.2.cloned.1.call-update) | async-done | bytes 3145744 | tf_op jit(solution)/shard_map/reduce_scatter | solution.py:62
  1306.9 5.1 add_convert_fusion
  (440 shorter events, 459.0 us)
Async XLA Ops:
  6.5 393.6 %all-gather.2.cloned.1.call-start = ((), (), s32[]{:S(2)}) async-start(), calls=%async_computation.2 | async-start | bytes 17301504 | tf_op jit(solution)/shard_map/all_gather | solution.py:41
  14.4 11.7 copy-start.2
  14.4 276.8 %all-to-all-start = ((bf16[32,1,256,1024]{2,3,1,0:T(8,128)(2,1)}), bf16[32,1,256,1024]{2,3,1,0:T(8,128)(2,1)}, u32[]{:S(2)}, u32[]{:S(2)}) async-start(bf16[32,1,256,1024]{2,3,1,0:T(8,128)(2,1)} %stack.2), calls=%async_computation | async-start | bytes 33554432 | tf_op jit(solution)/shard_map/all_to_all | solution.py:44
  26.0 1280.9 %reduce-scatter.2.cloned.1.call-start = ((), (), s32[]{:S(2)}) async-start(), calls=%async_computation.3 | async-start | bytes 15728640 | tf_op jit(solution)/shard_map/reduce_scatter | solution.py:62
  408.1 1.0 copy-start
  429.8 1.0 copy-start
  453.4 1.0 copy-start
  477.0 1.0 copy-start
  500.7 1.0 copy-start
  524.3 1.0 copy-start
  548.0 1.0 copy-start
  571.6 1.0 copy-start
  595.2 1.0 copy-start
  618.9 1.0 copy-start
  642.5 1.0 copy-start
  666.2 1.0 copy-start
  689.8 1.0 copy-start
  713.4 1.0 copy-start
  737.1 1.0 copy-start
  760.7 1.0 copy-start
  784.4 1.0 copy-start
  808.0 1.0 copy-start
  831.7 1.0 copy-start
  855.3 1.0 copy-start
  878.9 1.0 copy-start
  902.6 1.0 copy-start
  926.2 1.0 copy-start
  949.9 1.0 copy-start
  973.5 1.0 copy-start
  997.1 1.0 copy-start
  1020.8 1.0 copy-start
  1044.4 1.0 copy-start
  1068.1 1.0 copy-start
  1091.7 1.0 copy-start
  1115.3 1.0 copy-start
  1139.0 1.0 copy-start
  1179.6 127.3 %copy-start.1 = (bf16[1536,1024]{1,0:T(8,128)(2,1)S(1)}, bf16[1536,1024]{1,0:T(8,128)(2,1)}, u32[]{:S(2)}) copy-start(bf16[1536,1024]{1,0:T(8,128)(2,1)} %param.13) | copy-start | bytes 9437188
Sparse Core Ops, SparseCore 0:
  10.4 389.6 all-gather.1
  1179.7 127.1 reduce-scatter.1
